TPU v7x, 32 devices: a whole 2x2x4 slice. The times are simulated.
32 devices in a mesh: section: 8 (over y, x, core), tensor: 4 (over z).
Axes of the slice: x: 2, y: 2, z: 4, core: 2. Of those that a mesh axis runs over, the one named last changes fastest.
Arguments:
- states: bfloat16 [4096, 8192], P('section', 'tensor'), may hold values from -6 to 6
- lengths: int32 [8, 16], P('section'), may hold values from 1 to 96, 512 in all within a row
- routes: int32 [4096, 1], P('section'), may hold values from 0 to 7; in each aligned block of 512 rows (0 to 511, 512 to 1023, ...) at most 128 rows name the same one
- score_gain: float32 [8, 8192], P('section'), may hold values from 0.25 to 1.75
- score_weight: bfloat16 [8, 8192, 4096], P('section', None, 'tensor'), may hold values from -0.0625 to 0.0625
- score_heads: float32 [8, 4096, 2], P('section', 'tensor'), may hold values from -0.09375 to 0.09375
- actor_gain: float32 [8192], replicated, may hold values from 0.25 to 1.75
- actor_weight: bfloat16 [8192, 4096], P(None, 'tensor'), may hold values from -0.0625 to 0.0625
- actor_heads: float32 [4096], P('tensor'), may hold values from -0.09375 to 0.09375
Outputs:
- packed_scores: float32 [2, 8192], P(None, 'section')
- advantages: float32 [4096], P('section')
- actor_grad: float32 [8192, 4096], P('section', 'tensor')
Inputs may be any that keep to these rules, and one draw needn't show every extreme that they name: `lengths`: each row sums to 512; its largest entry is exactly 96. `routes`: in the rows of one section (aligned blocks of 512 rows) no member is named by more than 128 rows; some member is named by exactly 128 rows of some block.
All inputs are finite; a program needn't handle non-finite values.
Results may differ from a plain program's by a relative error of at most 0.0055.
Values may be sent and summed in bfloat16 or wider, within the bound.
A program may use at most 128 MiB of HBM per device.

v0:
```python
import jax
import jax.numpy as jnp
from jax import lax
from jax.sharding import PartitionSpec as P

epsilon = 1e-05
trace_decay = 0.95
penalty = 0.1


def compose(earlier, later):
    return (earlier[0] * later[0], later[1] + later[0] * earlier[1])


def advantage_rows(values, rewards, lengths):
    ends = jnp.cumsum(lengths, axis=1) - 1
    steps_idx = jnp.arange(values.shape[1], dtype=jnp.int32)
    last = jnp.any(steps_idx[None, :, None] == ends[:, None, :], axis=2)
    following = jnp.concatenate([values[:, 1:], jnp.zeros_like(values[:, :1])], axis=1)
    delta = jnp.where(last, rewards, following) - values
    weight = jnp.where(last, 0.0, trace_decay).astype(values.dtype)
    carried = lax.associative_scan(compose, (weight[:, ::-1], delta[:, ::-1]), axis=1)
    return carried[1][:, ::-1]


def body(
    states,
    lengths,
    routes,
    score_gain,
    score_weight,
    score_heads,
    actor_gain,
    actor_weight,
    actor_heads,
):
    sections = lax.axis_size("section")
    tok_count = states.shape[0]
    feat_shard = states.shape[1]
    capacity = 2 * tok_count // sections
    slot_count = sections * capacity
    target = routes[:, 0]
    onehot = (target[:, None] == jnp.arange(sections, dtype=jnp.int32)[None, :]).astype(jnp.int32)
    before = jnp.cumsum(onehot, axis=0) - onehot
    placed = jnp.sum(before * onehot, axis=1)
    slot_index = target * capacity + placed
    dispatch = (jnp.arange(slot_count, dtype=jnp.int32)[:, None] == slot_index[None, :]).astype(
        jnp.bfloat16
    )
    outbox = jnp.dot(dispatch, states, preferred_element_type=jnp.float32).astype(jnp.bfloat16)
    outbox = outbox.reshape(sections, capacity, feat_shard)
    arrived = lax.all_to_all(outbox, "section", split_axis=0, concat_axis=0, tiled=True).reshape(
        slot_count, feat_shard
    )
    gain_row = score_gain[0]
    member_weight = score_weight[0]
    feat_width = gain_row.shape[0]
    widened = lax.all_gather(arrived, "tensor", axis=1, tiled=True).astype(jnp.float32)
    scaled = (widened * gain_row[None, :]).astype(jnp.bfloat16)
    acc_total = jnp.dot(scaled, member_weight, preferred_element_type=jnp.float32)
    acc_total, squares = (acc_total, jnp.sum(widened * widened, axis=1))
    member_scale = lax.rsqrt(squares / feat_width + epsilon)
    preact = acc_total * member_scale[:, None]
    partial_scores = jnp.dot(jax.nn.silu(preact), score_heads[0], precision=lax.Precision.HIGHEST)
    scores = lax.psum(partial_scores, "tensor")
    packed_scores = jnp.transpose(scores)
    returned = lax.all_to_all(
        scores.reshape(sections, capacity, 2), "section", split_axis=0, concat_axis=0, tiled=True
    )
    returned = returned.reshape(slot_count, 2)
    token_scores = jnp.take(returned, slot_index, axis=0)
    raw_adv = advantage_rows(token_scores[:, 0][None, :], token_scores[:, 1][None, :], lengths)[0]
    adv_total, adv_square = lax.psum((jnp.sum(raw_adv), jnp.sum(raw_adv * raw_adv)), "section")
    total_tokens = tok_count * sections
    center = adv_total / total_tokens
    spread = adv_square / total_tokens - center * center
    advantages = (raw_adv - center) * lax.rsqrt(spread + epsilon)
    features = lax.all_gather(states, "tensor", axis=1, tiled=True)
    widened = features.astype(jnp.float32)
    actor_scale = lax.rsqrt(jnp.mean(widened * widened, axis=1) + epsilon)
    gained = (widened * actor_gain[None, :]).astype(jnp.bfloat16)
    actor_pre = (
        jnp.dot(gained, actor_weight, preferred_element_type=jnp.float32) * actor_scale[:, None]
    )
    shift_part = jnp.dot(jax.nn.silu(actor_pre), actor_heads, precision=lax.Precision.HIGHEST)
    log_shift = lax.psum(shift_part, "tensor")
    ratios = jnp.exp(log_shift)
    logit_slope = penalty * (ratios - 1.0) - ratios * advantages
    sigmoid_pre = jax.nn.sigmoid(actor_pre)
    silu_slope = sigmoid_pre * (1.0 + actor_pre * (1.0 - sigmoid_pre))
    grad_pre = ((logit_slope * actor_scale)[:, None] * actor_heads[None, :] * silu_slope).astype(
        jnp.bfloat16
    )
    blocks = lax.all_to_all(gained, "section", split_axis=1, concat_axis=0, tiled=True)
    every_row = lax.all_gather(grad_pre, "section", axis=0, tiled=True)
    actor_grad = lax.dot_general(
        blocks, every_row, (((0,), (0,)), ((), ())), preferred_element_type=jnp.float32
    )
    return (packed_scores, advantages, actor_grad)


def solution(mesh):
    in_specs = (
        P("section", "tensor"),
        P("section", None),
        P("section", None),
        P("section", None),
        P("section", None, "tensor"),
        P("section", "tensor", None),
        P(),
        P(None, "tensor"),
        P("tensor"),
    )
    out_specs = (P(None, "section"), P("section"), P("section", "tensor"))
    return jax.shard_map(body, mesh=mesh, in_specs=in_specs, out_specs=out_specs, check_vma=False)
```

profile of v0, /device:TPU:0, one launch (start us, length us, event | category | flops | bytes accessed | tf_op | source)
XLA Modules:
  0.0 717.2 jit_solution(90734786162934419)
XLA Ops:
  7.2 4.1 copy.28
  11.4 1.1 reduce-window.14
  12.9 2.4 convolution_convert_fusion
  15.3 54.1 %all_to_all.29 = bf16[8,128,2048]{2,1,0:T(8,128)(2,1)} all-to-all(bf16[8,128,2048]{2,1,0:T(8,128)(2,1)S(1)} %bitcast.52), channel_id=1, replica_groups=mesh['section'=8,'tensor'=4] {'section'}, dimensions={0} | all-to-all | bytes 8388608 | tf_op jit(solution)/shard_map/all_to_all | solution.py:52
  69.5 0.6 copy-done.8
  70.4 93.4 %all-gather.6.cloned.1.call-done = bf16[512,8192]{0,1:T(8,128)(2,1)} async-done(((bf16[512,2048]{0,1:T(8,128)(2,1)}), bf16[512,8192]{0,1:T(8,128)(2,1)}) %all-gather.6.cloned.1.call-update) | async-done | bytes 8388624 | tf_op jit(solution)/shard_map/all_gather | solution.py:78
  163.8 5.2 fusion.3
  169.1 15.5 %fusion.43 = f32[512,1024]{1,0:T(8,128)S(1)} fusion(bf16[512,8192]{0,1:T(8,128)(2,1)S(1)} %get-tuple-element.14, bf16[8192,1024]{1,0:T(8,128)(2,1)} %param.16), kind=kOutput, calls=%fused_computation.95 | convolution fusion | flops 8589934592 | bytes 27262976 | tf_op jit(solution)/shard_map/dot_general | solution.py:83
  184.6 2.4 fusion.15
  187.0 263.4 %all-gather.4.cloned.1.call-done = bf16[1024,8192]{1,0:T(8,128)(2,1)} async-done(((bf16[1024,2048]{1,0:T(8,128)(2,1)}), bf16[1024,8192]{1,0:T(8,128)(2,1)}) %all-gather.4.cloned.1.call-update) | async-done | bytes 16777232 | tf_op jit(solution)/shard_map/all_gather | solution.py:58
  450.4 7.5 %fusion.1 = f32[1024]{0:T(1024)S(1)} fusion(bf16[1024,8192]{1,0:T(8,128)(2,1)} %all-gather.4.cloned.1.call-done), kind=kLoop, calls=%fused_computation.4 | loop fusion | flops 25164800 | bytes 16781312 | tf_op jit(solution)/shard_map/reduce_sum | solution.py:61
  457.9 3.1 copy-done.2
  461.0 21.0 %fusion.4 = f32[1024,1024]{1,0:T(8,128)S(1)} fusion(bf16[1024,8192]{1,0:T(8,128)(2,1)S(1)} %copy-done.2, bf16[1,8192,1024]{2,1,0:T(8,128)(2,1)} %param.13, f32[8192]{0:T(1024)S(1)} %bitcast.73), kind=kOutput, calls=%fused_computation.9 | convolution fusion | flops 17205035008 | bytes 37781504 | tf_op jit(solution)/shard_map/dot_general | solution.py:60
  482.1 4.5 fusion.8
  486.6 16.3 %all-reduce.19 = (f32[1024,2]{0,1:T(2,128)}, f32[512]{0:T(512)S(1)}) all-reduce(f32[1024,2]{0,1:T(2,128)S(1)} %fusion.8, f32[512]{0:T(512)S(1)} %bitcast.66), channel_id=1, replica_groups=mesh['section'=8,'tensor'=4] {'tensor'}, use_global_device_ids=true, to_apply=%region_4.5 | all-reduce | flops 2560 | bytes 20480 | tf_op jit(solution)/shard_map/psum | solution.py:65
  502.8 3.9 all-to-all-start.1
  506.8 4.7 all-to-all-done.1
  511.4 0.2 copy.27
  511.6 1.0 gather_fusion
  512.8 0.3 slice_reduce_fusion.1
  513.3 0.2 slice.259
  513.5 0.2 slice.253
  513.7 0.2 slice.251
  514.0 0.2 slice.255
  514.9 0.2 slice.267
  515.2 0.2 slice.263
  515.4 0.2 slice.262
  515.6 0.2 slice.264
  519.4 0.7 slice.303
  520.3 0.6 fusion.34
  521.0 0.2 slice.258
  521.3 0.2 slice.261
  521.5 0.5 slice.326
  522.2 0.2 slice.247
  522.4 0.6 slice.325
  523.1 0.6 fusion.36
  523.7 0.6 slice.310
  526.2 0.7 pad_add_fusion
  528.3 0.7 pad_maximum_fusion.1
  531.0 0.6 pad_maximum_fusion.7
  532.3 0.7 pad_maximum_fusion
  533.5 0.4 rev.2
  533.8 0.6 fusion.32
  534.5 12.7 %all-reduce.18 = (f32[]{:T(128)}, f32[]{:T(128)}) all-reduce(f32[]{:T(128)} %get-tuple-element.6, f32[]{:T(128)} %get-tuple-element.5), channel_id=1, replica_groups=mesh['section'=8,'tensor'=4] {'section'}, use_global_device_ids=true, to_apply=%region_10.11 | all-reduce | flops 2 | bytes 16 | tf_op jit(solution)/shard_map/psum | solution.py:73
  549.8 1.9 multiply_convert_fusion
  551.7 132.4 %all_to_all.30 = bf16[512,8,1024]{0,2,1:T(8,128)(2,1)} all-to-all(bf16[512,8,1024]{0,2,1:T(8,128)(2,1)} %bitcast.47), channel_id=1, replica_groups=mesh['section'=8,'tensor'=4] {'section'}, dimensions={1} | all-to-all | bytes 16777216 | tf_op jit(solution)/shard_map/all_to_all | solution.py:94
  684.1 11.5 %copy.29 = bf16[8,512,1024]{2,1,0:T(8,128)(2,1)} copy(bf16[8,512,1024]{1,2,0:T(8,128)(2,1)} %bitcast.48) | data formatting | bytes 16777216 | tf_op jit(solution)/shard_map/all_to_all | solution.py:94
  695.6 15.0 %fusion.44 = f32[1024,1024]{1,0:T(8,128)} fusion(bf16[4096,1024]{1,0:T(8,128)(2,1)} %bitcast.51, bf16[4096,1024]{1,0:T(8,128)(2,1)} %all-gather.8.cloned.1.call-done), kind=kOutput, calls=%fused_computation.96 | convolution fusion | flops 8589934592 | bytes 20971520 | tf_op jit(solution)/shard_map/dot_general | solution.py:96
  (129 shorter events, 9.2 us)
Async XLA Ops:
  7.2 474.9 %copy-start = (f32[1,1024,2]{1,2,0:T(2,128)S(1)}, f32[1,1024,2]{1,2,0:T(2,128)}, u32[]{:S(2)}) copy-start(f32[1,1024,2]{1,2,0:T(2,128)} %param.14) | copy-start | bytes 24580
  7.2 5.7 copy-start.3
  7.2 4.2 copy-start.5
  7.2 156.6 %all-gather.6.cloned.1.call-start = ((), (), s32[]{:S(2)}) async-start(), calls=%async_computation.4 | async-start | bytes 10485760 | tf_op jit(solution)/shard_map/all_gather | solution.py:78
  11.3 439.0 %all-gather.4.cloned.1.call-start = ((), (), s32[]{:S(2)}) async-start(), calls=%async_computation.3 | async-start | bytes 20971520 | tf_op jit(solution)/shard_map/all_gather | solution.py:58
  69.4 0.7 copy-start.8
  69.4 94.4 %copy-start.4 = (f32[8192]{0:T(1024)S(1)}, f32[8192]{0:T(1024)}, u32[]{:S(2)}) copy-start(f32[8192]{0:T(1024)} %param.15) | copy-start | bytes 98308
  169.1 15.5 %copy-start.1 = (bf16[512,8192]{0,1:T(8,128)(2,1)}, bf16[512,8192]{0,1:T(8,128)(2,1)S(1)}, u32[]{:S(2)}) copy-start(bf16[512,8192]{0,1:T(8,128)(2,1)S(1)} %get-tuple-element.14) | copy-start | bytes 25165828
  169.1 15.5 %copy-start.7 = (f32[1024]{0:T(1024)S(1)}, f32[1024]{0:T(1024)}, u32[]{:S(2)}) copy-start(f32[1024]{0:T(1024)} %param.17) | copy-start | bytes 12292
  184.6 273.3 %copy-start.9 = (f32[1,8192]{1,0:T(1,128)S(1)}, f32[1,8192]{1,0:T(1,128)}, u32[]{:S(2)}) copy-start(f32[1,8192]{1,0:T(1,128)} %param.12) | copy-start | bytes 98308
  450.4 10.7 %copy-start.2 = (bf16[1024,8192]{1,0:T(8,128)(2,1)S(1)}, bf16[1024,8192]{1,0:T(8,128)(2,1)}, u32[]{:S(2)}) copy-start(bf16[1024,8192]{1,0:T(8,128)(2,1)} %all-gather.4.cloned.1.call-done) | copy-start | bytes 50331652
  502.8 8.6 %all-to-all-start.1 = ((f32[8,128,2]{1,2,0:T(2,128)}), f32[8,128,2]{1,2,0:T(2,128)S(1)}, u32[]{:S(2)}, u32[]{:S(2)}) async-start(f32[8,128,2]{1,2,0:T(2,128)} %bitcast.12), calls=%async_computation.1 | async-start | bytes 16384 | tf_op jit(solution)/shard_map/all_to_all | solution.py:67
  506.7 188.9 %all-gather.8.cloned.1.call-start = ((), (), s32[]{:S(2)}) async-start(), calls=%async_computation.5 | async-start | bytes 9437184 | tf_op jit(solution)/shard_map/all_gather | solution.py:95
  549.8 134.4 %copy-start.6 = (f32[1,512]{1,0:T(1,128)}, f32[1,512]{1,0:T(1,128)S(1)}, u32[]{:S(2)}) copy-start(f32[1,512]{1,0:T(1,128)S(1)} %subtract_multiply_fusion.1) | copy-start | bytes 6148
Sparse Core Ops, SparseCore 0:
  11.5 152.3 all-gather.5
  165.4 284.9 all-gather.3
  551.8 119.5 all-gather.7
where the time goes:
time: 718 us; the launch traced here: 717 us
  waiting for transfers between devices  361 us (50%)
  blocking collectives  215 us (30%)
  matrix products  60.8 us (8%)
  local copies, waits for them, and re-layouts  35 us (5%)
  other arithmetic  20.5 us (3%)
  between operations  20 us (3%)
    all_gather x1, waiting for transfers between devices, body(): lax.all_gather(arrived, 'tensor', axis=1, tiled=True).astype(jnp.float32)  263 us
    all_to_all x1, blocking collectives, body(): lax.all_to_all(gained, 'section', split_axis=1, concat_axis=0, tiled=True)  132 us
    all_gather x1, waiting for transfers between devices, body(): features = lax.all_gather(states, 'tensor', axis=1, tiled=True)  93.4 us
    all_to_all x1, blocking collectives, body(): lax.all_to_all(outbox, 'section', split_axis=0, concat_axis=0, tiled=True)  54.1 us
    dot_general x1, matrix products, body(): jnp.dot(scaled, member_weight, preferred_element_type=jnp.float32)  21 us
    psum x1, blocking collectives, body(): scores = lax.psum(partial_scores, 'tensor')  16.3 us
    dot_general x1, matrix products, body(): jnp.dot(gained, actor_weight, preferred_element_type=jnp.float32)  15.5 us
    dot_general x1, matrix products, body(): lax.dot_general(blocks, every_row, (((0,), (0,)), ((), ())), preferred_el...  15 us
  transfers between devices with their start and end apart: 4, of which 3 were waited for; matrix products, arithmetic and copies ran while one was open for 5% of the time, Pallas kernels for 0%

commit v1 on v0

--- a/solution.py
+++ b/solution.py
@@ -75,7 +75,27 @@
     center = adv_total / total_tokens
     spread = adv_square / total_tokens - center * center
     advantages = (raw_adv - center) * lax.rsqrt(spread + epsilon)
-    features = lax.all_gather(states, "tensor", axis=1, tiled=True)
+    incoming_x = states
+    q_next, v1, even = (
+        lax.psum(1, axis_name="tensor"),
+        lax.axis_index("tensor"),
+        incoming_x.shape[1],
+    )
+    shelf = [i * q_next if tick == 1 else i for tick, i in enumerate(incoming_x.shape)]
+    features = lax.dynamic_update_slice_in_dim(
+        jnp.zeros(shelf, incoming_x.dtype), incoming_x, v1 * even, axis=1
+    )
+    j = 1
+    while j < q_next:
+        incoming_x = lax.ppermute(
+            incoming_x,
+            axis_name="tensor",
+            perm=[(tick, (tick + 1) % q_next) for tick in range(q_next)],
+        )
+        features = lax.dynamic_update_slice_in_dim(
+            features, incoming_x, (v1 - j) % q_next * even, axis=1
+        )
+        j += 1
     widened = features.astype(jnp.float32)
     actor_scale = lax.rsqrt(jnp.mean(widened * widened, axis=1) + epsilon)
     gained = (widened * actor_gain[None, :]).astype(jnp.bfloat16)

time: 718 us -> 769 us (1.071)
  starting transfers between devices: 3.98 us -> 102 us
  waiting for transfers between devices: 361 us -> 287 us
  blocking collectives: 215 us -> 236 us
    ppermute x0 -> x3, waiting for transfers between devices: none -> 254 us  [body(): lax.ppermute(incoming_x, axis_name='tensor', perm=[(tick, (tick + 1) % q_...]
    all_gather x1, waiting for transfers between devices: 263 us -> 28.9 us  [body(): lax.all_gather(arrived, 'tensor', axis=1, tiled=True).astype(jnp.float32)]
    ppermute x0 -> x3, starting transfers between devices: none -> 98.4 us  [body(): lax.ppermute(incoming_x, axis_name='tensor', perm=[(tick, (tick + 1) % q_...]
    all_gather x1 -> x0, waiting for transfers between devices: 93.4 us -> none  [body(): features = lax.all_gather(states, 'tensor', axis=1, tiled=True)]
    psum x1, blocking collectives: 16.3 us -> 37.1 us  [body(): scores = lax.psum(partial_scores, 'tensor')]
  transfers between devices with their start and end apart: 4 -> 6, of which waited for: 3 -> 5; matrix products, arithmetic and copies ran while one was open for 5% -> 5% of each run, Pallas kernels for 0% -> 0%
where the time goes in v1:
time: 769 us; the launch traced here: 768 us
  waiting for transfers between devices  287 us (37%)
  blocking collectives  236 us (31%)
  starting transfers between devices  102 us (13%)
  matrix products  61.8 us (8%)
  local copies, waits for them, and re-layouts  40.5 us (5%)
  between operations  20.3 us (3%)
  other arithmetic  19.9 us (3%)
    ppermute x3, waiting for transfers between devices, body(): lax.ppermute(incoming_x, axis_name='tensor', perm=[(tick, (tick + 1) % q_...  254 us
    all_to_all x1, blocking collectives, body(): lax.all_to_all(gained, 'section', split_axis=1, concat_axis=0, tiled=True)  132 us
    ppermute x3, starting transfers between devices, body(): lax.ppermute(incoming_x, axis_name='tensor', perm=[(tick, (tick + 1) % q_...  98.4 us
    all_to_all x1, blocking collectives, body(): lax.all_to_all(outbox, 'section', split_axis=0, concat_axis=0, tiled=True)  54.1 us
    psum x1, blocking collectives, body(): scores = lax.psum(partial_scores, 'tensor')  37.1 us
    all_gather x1, waiting for transfers between devices, body(): lax.all_gather(arrived, 'tensor', axis=1, tiled=True).astype(jnp.float32)  28.9 us
    dot_general x1, matrix products, body(): jnp.dot(scaled, member_weight, preferred_element_type=jnp.float32)  21 us
  transfers between devices with their start and end apart: 6, of which 5 were waited for; matrix products, arithmetic and copies ran while one was open for 5% of the time, Pallas kernels for 0%

profile of v1, /device:TPU:0, one launch (start us, length us, event | category | flops | bytes accessed | tf_op | source)
XLA Modules:
  0.0 768.0 jit_solution(395803632757429264)
XLA Ops:
  7.2 0.7 fusion.26
  7.9 1.1 reduce-window.14
  9.3 0.8 fusion.25
  10.1 0.7 multiply_add_fusion
  10.8 3.9 convolution_convert_fusion
  14.7 54.1 %all_to_all.29 = bf16[8,128,2048]{2,1,0:T(8,128)(2,1)} all-to-all(bf16[8,128,2048]{2,1,0:T(8,128)(2,1)S(1)} %bitcast.52), channel_id=1, replica_groups=mesh['section'=8,'tensor'=4] {'section'}, dimensions={0} | all-to-all | bytes 8388608 | tf_op jit(solution)/shard_map/all_to_all | solution.py:52
  68.9 2.9 copy.30
  71.7 1.6 collective-permute-start
  73.4 84.6 %collective-permute-done = bf16[512,2048]{0,1:T(8,128)(2,1)S(1)} collective-permute-done((bf16[512,2048]{0,1:T(8,128)(2,1)S(1)}, bf16[512,2048]{0,1:T(8,128)(2,1)S(1)}, u32[]{:S(2)}, u32[]{:S(2)}) %collective-permute-start) | collective-permute-done | bytes 2097184 | tf_op jit(solution)/shard_map/ppermute | solution.py:90
  157.9 1.3 copy-done.3
  159.2 43.0 %collective-permute-start.1 = (bf16[512,2048]{0,1:T(8,128)(2,1)S(1)}, bf16[512,2048]{0,1:T(8,128)(2,1)}, u32[]{:S(2)}, u32[]{:S(2)}) collective-permute-start(bf16[512,2048]{0,1:T(8,128)(2,1)S(1)} %collective-permute-done), channel_id=1, source_target_pairs={{0,1},{1,2},{2,3},{3,0},{4,5},{5,6},{6,7},{7,4},{8,9},{9,10},{10,1... | collective-permute-start | bytes 6291464 | tf_op jit(solution)/shard_map/ppermute | solution.py:90
  202.3 85.7 %collective-permute-done.1 = bf16[512,2048]{0,1:T(8,128)(2,1)} collective-permute-done((bf16[512,2048]{0,1:T(8,128)(2,1)S(1)}, bf16[512,2048]{0,1:T(8,128)(2,1)}, u32[]{:S(2)}, u32[]{:S(2)}) %collective-permute-start.1) | collective-permute-done | bytes 2097184 | tf_op jit(solution)/shard_map/ppermute | solution.py:90
  288.0 53.7 %collective-permute-start.2 = (bf16[512,2048]{0,1:T(8,128)(2,1)}, bf16[512,2048]{0,1:T(8,128)(2,1)}, u32[]{:S(2)}, u32[]{:S(2)}) collective-permute-start(bf16[512,2048]{0,1:T(8,128)(2,1)} %collective-permute-done.1), channel_id=1, source_target_pairs={{0,1},{1,2},{2,3},{3,0},{4,5},{5,6},{6,7},{7,4},{8,9},{9,10},{10,1... | collective-permute-start | bytes 6291464 | tf_op jit(solution)/shard_map/ppermute | solution.py:90
  342.0 0.5 broadcast_in_dim.35
  342.9 1.3 copy-done.4
  344.5 1.8 constant_dynamic-update-slice_fusion.1
  346.3 83.7 %collective-permute-done.2 = bf16[512,2048]{0,1:T(8,128)(2,1)} collective-permute-done((bf16[512,2048]{0,1:T(8,128)(2,1)}, bf16[512,2048]{0,1:T(8,128)(2,1)}, u32[]{:S(2)}, u32[]{:S(2)}) %collective-permute-start.2) | collective-permute-done | bytes 2097184 | tf_op jit(solution)/shard_map/ppermute | solution.py:90
  429.9 1.8 constant_dynamic-update-slice_fusion
  431.8 2.6 fusion.3
  434.4 14.9 %fusion.43 = f32[512,1024]{1,0:T(8,128)S(1)} fusion(bf16[512,8192]{0,1:T(8,128)(2,1)S(1)} %get-tuple-element.14, bf16[8192,1024]{1,0:T(8,128)(2,1)} %param.16), kind=kOutput, calls=%fused_computation.99 | convolution fusion | flops 8589934592 | bytes 27262976 | tf_op jit(solution)/shard_map/dot_general | solution.py:103
  449.3 2.4 fusion.15
  451.7 28.9 %all-gather.3.cloned.1.call-done = bf16[1024,8192]{1,0:T(8,128)(2,1)} async-done(((bf16[1024,2048]{1,0:T(8,128)(2,1)}), bf16[1024,8192]{1,0:T(8,128)(2,1)}) %all-gather.3.cloned.1.call-update) | async-done | bytes 16777232 | tf_op jit(solution)/shard_map/all_gather | solution.py:58
  480.6 7.5 fusion.1
  488.1 3.1 copy-done.2
  491.3 21.0 %fusion.4 = f32[1024,1024]{1,0:T(8,128)S(1)} fusion(bf16[1024,8192]{1,0:T(8,128)(2,1)S(1)} %copy-done.2, bf16[1,8192,1024]{2,1,0:T(8,128)(2,1)} %param.13, f32[8192]{0:T(1024)S(1)} %bitcast.73), kind=kOutput, calls=%fused_computation.9 | convolution fusion | flops 17205035008 | bytes 37781504 | tf_op jit(solution)/shard_map/dot_general | solution.py:60
  512.3 4.5 fusion.8
  516.8 37.1 %all-reduce.19 = (f32[1024,2]{0,1:T(2,128)}, f32[512]{0:T(512)S(1)}) all-reduce(f32[1024,2]{0,1:T(2,128)S(1)} %fusion.8, f32[512]{0:T(512)S(1)} %bitcast.66), channel_id=1, replica_groups=mesh['section'=8,'tensor'=4] {'tensor'}, use_global_device_ids=true, to_apply=%region_4.5 | all-reduce | flops 2560 | bytes 20480 | tf_op jit(solution)/shard_map/psum | solution.py:65
  554.0 3.3 all-to-all-start.1
  557.4 4.6 all-to-all-done.1
  562.2 1.0 gather_fusion
  563.4 0.3 slice_reduce_fusion.1
  569.9 0.7 slice.303
  570.8 0.6 fusion.34
  572.0 0.5 slice.326
  573.0 0.6 slice.325
  573.6 0.6 fusion.36
  574.2 0.6 slice.310
  576.7 0.7 pad_add_fusion
  578.8 0.7 pad_maximum_fusion.1
  581.5 0.6 pad_maximum_fusion.7
  582.8 0.7 pad_maximum_fusion
  584.0 0.4 rev.2
  584.4 0.6 fusion.32
  585.0 12.6 %all-reduce.18 = (f32[]{:T(128)}, f32[]{:T(128)}) all-reduce(f32[]{:T(128)} %get-tuple-element.6, f32[]{:T(128)} %get-tuple-element.5), channel_id=1, replica_groups=mesh['section'=8,'tensor'=4] {'section'}, use_global_device_ids=true, to_apply=%region_10.11 | all-reduce | flops 2 | bytes 16 | tf_op jit(solution)/shard_map/psum | solution.py:73
  600.3 1.9 multiply_convert_fusion
  602.2 132.5 %all_to_all.30 = bf16[512,8,1024]{0,2,1:T(8,128)(2,1)} all-to-all(bf16[512,8,1024]{0,2,1:T(8,128)(2,1)} %bitcast.47), channel_id=1, replica_groups=mesh['section'=8,'tensor'=4] {'section'}, dimensions={1} | all-to-all | bytes 16777216 | tf_op jit(solution)/shard_map/all_to_all | solution.py:114
  734.7 11.5 %copy.32 = bf16[8,512,1024]{2,1,0:T(8,128)(2,1)} copy(bf16[8,512,1024]{1,2,0:T(8,128)(2,1)} %bitcast.48) | data formatting | bytes 16777216 | tf_op jit(solution)/shard_map/all_to_all | solution.py:114
  746.2 15.0 %fusion.44 = f32[1024,1024]{1,0:T(8,128)} fusion(bf16[4096,1024]{1,0:T(8,128)(2,1)} %bitcast.51, bf16[4096,1024]{1,0:T(8,128)(2,1)} %all-gather.5.cloned.1.call-done), kind=kOutput, calls=%fused_computation.100 | convolution fusion | flops 8589934592 | bytes 20971520 | tf_op jit(solution)/shard_map/dot_general | solution.py:116
  (139 shorter events, 12.3 us)
Async XLA Ops:
  7.2 505.1 %copy-start = (f32[1,1024,2]{1,2,0:T(2,128)S(1)}, f32[1,1024,2]{1,2,0:T(2,128)}, u32[]{:S(2)}) copy-start(f32[1,1024,2]{1,2,0:T(2,128)} %param.14) | copy-start | bytes 24580
  7.2 473.4 %all-gather.3.cloned.1.call-start = ((), (), s32[]{:S(2)}) async-start(), calls=%async_computation.3 | async-start | bytes 20971520 | tf_op jit(solution)/shard_map/all_gather | solution.py:58
  68.8 272.8 %copy-start.9 = (s32[1,16]{1,0:T(1,128)S(1)}, s32[1,16]{1,0:T(1,128)}, u32[]{:S(2)}) copy-start(s32[1,16]{1,0:T(1,128)} %param.10) | copy-start | bytes 196
  68.8 273.2 %copy-start.6 = (s32[512,1]{0,1:T(1,128)S(1)}, s32[512,1]{0,1:T(1,128)}, u32[]{:S(2)}) copy-start(s32[512,1]{0,1:T(1,128)} %param.11) | copy-start | bytes 6148
  71.7 86.2 %collective-permute-start = (bf16[512,2048]{0,1:T(8,128)(2,1)S(1)}, bf16[512,2048]{0,1:T(8,128)(2,1)S(1)}, u32[]{:S(2)}, u32[]{:S(2)}) collective-permute-start(bf16[512,2048]{0,1:T(8,128)(2,1)S(1)} %copy.30), channel_id=1, source_target_pairs={{0,1},{1,2},{2,3},{3,0},{4,5},{5,6},{6,7},{7,4},{8,9},{9,10},{10,1... | collective-permute-start | bytes 6291464 | tf_op jit(solution)/shard_map/ppermute | solution.py:90
  157.9 1.3 copy-start.3
  159.2 128.7 %collective-permute-start.1 = (bf16[512,2048]{0,1:T(8,128)(2,1)S(1)}, bf16[512,2048]{0,1:T(8,128)(2,1)}, u32[]{:S(2)}, u32[]{:S(2)}) collective-permute-start(bf16[512,2048]{0,1:T(8,128)(2,1)S(1)} %collective-permute-done), channel_id=1, source_target_pairs={{0,1},{1,2},{2,3},{3,0},{4,5},{5,6},{6,7},{7,4},{8,9},{9,10},{10,1... | collective-permute-start | bytes 6291464 | tf_op jit(solution)/shard_map/ppermute | solution.py:90
  288.0 142.0 %collective-permute-start.2 = (bf16[512,2048]{0,1:T(8,128)(2,1)}, bf16[512,2048]{0,1:T(8,128)(2,1)}, u32[]{:S(2)}, u32[]{:S(2)}) collective-permute-start(bf16[512,2048]{0,1:T(8,128)(2,1)} %collective-permute-done.1), channel_id=1, source_target_pairs={{0,1},{1,2},{2,3},{3,0},{4,5},{5,6},{6,7},{7,4},{8,9},{9,10},{10,1... | collective-permute-start | bytes 6291464 | tf_op jit(solution)/shard_map/ppermute | solution.py:90
  342.6 1.6 copy-start.4
  344.4 87.3 %copy-start.5 = (f32[8192]{0:T(1024)S(1)}, f32[8192]{0:T(1024)}, u32[]{:S(2)}) copy-start(f32[8192]{0:T(1024)} %param.15) | copy-start | bytes 98308
  434.3 15.0 %copy-start.1 = (bf16[512,8192]{0,1:T(8,128)(2,1)}, bf16[512,8192]{0,1:T(8,128)(2,1)S(1)}, u32[]{:S(2)}) copy-start(bf16[512,8192]{0,1:T(8,128)(2,1)S(1)} %get-tuple-element.14) | copy-start | bytes 25165828
  434.3 14.9 %copy-start.8 = (f32[1024]{0:T(1024)S(1)}, f32[1024]{0:T(1024)}, u32[]{:S(2)}) copy-start(f32[1024]{0:T(1024)} %param.17) | copy-start | bytes 12292
  449.3 38.8 %copy-start.10 = (f32[1,8192]{1,0:T(1,128)S(1)}, f32[1,8192]{1,0:T(1,128)}, u32[]{:S(2)}) copy-start(f32[1,8192]{1,0:T(1,128)} %param.12) | copy-start | bytes 98308
  480.6 10.7 %copy-start.2 = (bf16[1024,8192]{1,0:T(8,128)(2,1)S(1)}, bf16[1024,8192]{1,0:T(8,128)(2,1)}, u32[]{:S(2)}) copy-start(bf16[1024,8192]{1,0:T(8,128)(2,1)} %all-gather.3.cloned.1.call-done) | copy-start | bytes 50331652
  554.0 8.0 %all-to-all-start.1 = ((f32[8,128,2]{1,2,0:T(2,128)}), f32[8,128,2]{1,2,0:T(2,128)S(1)}, u32[]{:S(2)}, u32[]{:S(2)}) async-start(f32[8,128,2]{1,2,0:T(2,128)} %bitcast.12), calls=%async_computation.1 | async-start | bytes 16384 | tf_op jit(solution)/shard_map/all_to_all | solution.py:67
  557.3 188.9 %all-gather.5.cloned.1.call-start = ((), (), s32[]{:S(2)}) async-start(), calls=%async_computation.4 | async-start | bytes 9437184 | tf_op jit(solution)/shard_map/all_gather | solution.py:115
  600.3 134.4 %copy-start.7 = (f32[1,512]{1,0:T(1,128)}, f32[1,512]{1,0:T(1,128)S(1)}, u32[]{:S(2)}) copy-start(f32[1,512]{1,0:T(1,128)S(1)} %subtract_multiply_fusion.1) | copy-start | bytes 6148
Sparse Core Ops, SparseCore 0:
  69.0 411.5 all-gather.2
  602.3 119.0 all-gather.4
